TPU v7x, 32 devices: a whole 2x2x4 slice. The times are simulated.
32 devices in a mesh: dp: 8 (over z, y), mp: 4 (over x, core).
Axes of the slice: x: 2, y: 2, z: 4, core: 2. Of those that a mesh axis runs over, the one named last changes fastest.
Arguments:
- x_in: bfloat16 [8192, 768], P(('dp', 'mp')), may hold values from -6 to 6
- out_grad: bfloat16 [8192, 768], P(('dp', 'mp')), may hold values from -6 to 6
- doc_lengths: int32 [8, 8], P('dp'), may hold values from 1 to 512, 1024 in all within a row
- keep_layer: int32 [8], P('dp'), may hold values 0 or 1
- w_qkv: float32 [2, 3, 768, 768], P(None, None, 'dp', 'mp'), may hold values from -0.21875 to 0.21875
- w_o: float32 [2, 768, 768], P(None, 'mp', 'dp'), may hold values from -0.625 to 0.625
- w_in: float32 [2, 768, 3072], P(None, 'dp', 'mp'), may hold values from -0.21875 to 0.21875
- w_out: float32 [2, 3072, 768], P(None, 'mp', 'dp'), may hold values from -0.109375 to 0.109375
- b_qv: float32 [2, 2, 768], P(None, None, 'mp'), may hold values from -1.2 to 1.2
- b_in: float32 [2, 3072], P(None, 'mp'), may hold values from -1.2 to 1.2
- ln_gain: float32 [2, 2, 768], replicated, may hold values from 0.5 to 1.5
- shifts: float32 [2, 4, 768], replicated, may hold values from -1.2 to 1.2
- m_qkv: float32 [2, 3, 768, 768], P(None, None, 'dp', 'mp'), may hold values from -3 to 3
- m_o: float32 [2, 768, 768], P(None, 'mp', 'dp'), may hold values from -3 to 3
- m_in: float32 [2, 768, 3072], P(None, 'dp', 'mp'), may hold values from -3 to 3
- m_out: float32 [2, 3072, 768], P(None, 'mp', 'dp'), may hold values from -3 to 3
- m_qv: float32 [2, 2, 768], P(None, None, 'mp'), may hold values from -6 to 6
- m_bin: float32 [2, 3072], P(None, 'mp'), may hold values from -6 to 6
- m_gain: float32 [2, 2, 768], replicated, may hold values from -6 to 6
- m_shift: float32 [2, 4, 768], replicated, may hold values from -6 to 6
- e_qkv: float32 [8, 2, 3, 768, 768], P('dp', None, None, None, 'mp'), may hold values from -30 to 30
- e_o: float32 [8, 2, 768, 768], P('dp', None, 'mp'), may hold values from -30 to 30
- e_in: float32 [8, 2, 768, 3072], P('dp', None, None, 'mp'), may hold values from -30 to 30
- e_out: float32 [8, 2, 3072, 768], P('dp', None, 'mp'), may hold values from -30 to 30
- q_qkv: float32 [2, 3, 768, 8], P(None, None, 'mp'), may hold values from -6 to 6
- q_o: float32 [2, 3072, 8], P(None, 'mp'), may hold values from -6 to 6
- q_in: float32 [2, 3072, 8], P(None, 'mp'), may hold values from -6 to 6
- q_out: float32 [2, 3072, 8], P(None, 'mp'), may hold values from -6 to 6
Outputs:
- block_output: float32 [8192, 768], P(('dp', 'mp'))
- input_gradient: float32 [8192, 768], P(('dp', 'mp'))
- new_w_qkv: float32 [2, 3, 768, 768], P(None, None, 'dp', 'mp')
- new_w_o: float32 [2, 768, 768], P(None, 'mp', 'dp')
- new_w_in: float32 [2, 768, 3072], P(None, 'dp', 'mp')
- new_w_out: float32 [2, 3072, 768], P(None, 'mp', 'dp')
- new_b_qv: float32 [2, 2, 768], P(None, None, 'mp')
- new_b_in: float32 [2, 3072], P(None, 'mp')
- new_gain: float32 [2, 2, 768], replicated
- new_shifts: float32 [2, 4, 768], replicated
- new_m_qkv: float32 [2, 3, 768, 768], P(None, None, 'dp', 'mp')
- new_m_o: float32 [2, 768, 768], P(None, 'mp', 'dp')
- new_m_in: float32 [2, 768, 3072], P(None, 'dp', 'mp')
- new_m_out: float32 [2, 3072, 768], P(None, 'mp', 'dp')
- new_m_qv: float32 [2, 2, 768], P(None, None, 'mp')
- new_m_bin: float32 [2, 3072], P(None, 'mp')
- new_m_gain: float32 [2, 2, 768], replicated
- new_m_shift: float32 [2, 4, 768], replicated
- new_e_qkv: float32 [8, 2, 3, 768, 768], P('dp', None, None, None, 'mp')
- new_e_o: float32 [8, 2, 768, 768], P('dp', None, 'mp')
- new_e_in: float32 [8, 2, 768, 3072], P('dp', None, None, 'mp')
- new_e_out: float32 [8, 2, 3072, 768], P('dp', None, 'mp')
- p_qkv: float32 [2, 3, 3072, 8], P(None, None, 'mp')
- p_o: float32 [2, 768, 8], P(None, 'mp')
- p_in: float32 [2, 3072, 8], P(None, 'mp')
- p_out: float32 [2, 3072, 8], P(None, 'mp')
- new_q_qkv: float32 [2, 3, 768, 8], P(None, None, 'mp')
- new_q_o: float32 [2, 3072, 8], P(None, 'mp')
- new_q_in: float32 [2, 3072, 8], P(None, 'mp')
- new_q_out: float32 [2, 3072, 8], P(None, 'mp')
Inputs may be any that keep to these rules, and one draw needn't show every extreme that they name: `doc_lengths`: each row holds the 8 document lengths of one replica, which sum to 1024; the longest document of every replica has exactly 512 tokens.
All inputs are finite; a program needn't handle non-finite values. No bound on the sum of `keep_layer` on one device may be relied on, other than what follows from the above.
Results may differ from a plain program's by a relative error of at most 0.02.
Values may be sent and summed in bfloat16 or wider, within the bound.
No kernel may reach another device: no remote copies, remote signals or barrier semaphores. Data moves between devices by JAX's collectives and lax.ppermute only.
A program may use at most 192 MiB of HBM per device.

v0:
```python
import jax
import jax.numpy as jnp
from jax import lax
from jax.sharding import PartitionSpec as P

HD = 64


NORM_EPS = 1e-05
ORTHO_EPS = 1e-06
MOMENTUM = 0.9
RATE = 0.05
MASKED = -1000000000.0
ROOT_HALF = 0.7071067811865476
INV_ROOT_TWO_PI = 0.3989422804014327
HIGHEST = lax.Precision.HIGHEST


def contract_rows(left, right):
    return lax.dot_general(
        left, right, (((0,), (0,)), ((), ())), preferred_element_type=jnp.float32
    )


def contract_cols(left, right):
    return lax.dot_general(
        left, right, (((1,), (1,)), ((), ())), preferred_element_type=jnp.float32
    )


def gelu_value(upper):
    return 0.5 * upper * (1.0 + lax.erf(upper * ROOT_HALF))


def gelu_slope(upper):
    return (
        0.5 * (1.0 + lax.erf(upper * ROOT_HALF))
        + upper * jnp.exp(-0.5 * upper * upper) * INV_ROOT_TWO_PI
    )


def norm_forward(rows_in, gain, shift):
    centred = rows_in - jnp.mean(rows_in, axis=-1, keepdims=True)
    inverse = lax.rsqrt(jnp.mean(centred * centred, axis=-1, keepdims=True) + NORM_EPS)
    normed = centred * inverse
    return (normed * gain + shift, normed, inverse)


def norm_backward(grad, normed, inverse, gain):
    scaled = grad * gain
    inner = jnp.mean(scaled * normed, axis=-1, keepdims=True)
    back = inverse * (scaled - jnp.mean(scaled, axis=-1, keepdims=True) - normed * inner)
    return (back, jnp.sum(grad * normed, axis=0), jnp.sum(grad, axis=0))


def doc_positions(lengths, count):
    ends = jnp.cumsum(lengths)
    places = jnp.arange(count, dtype=jnp.int32)
    return jnp.sum((places[:, None] >= ends[None, :]).astype(jnp.int32), axis=1)


def orthogonal(factor):
    rank = factor.shape[-1]
    for column in range(rank):
        vector = factor[..., column : column + 1]
        vector = vector * lax.rsqrt(jnp.sum(vector * vector, axis=-2, keepdims=True) + ORTHO_EPS)
        remain = factor[..., column + 1 :]
        remain = remain - vector * jnp.sum(vector * remain, axis=-2, keepdims=True)
        factor = jnp.concatenate([factor[..., :column], vector, remain], axis=-1)
    return factor


def attend(query, keys, values, docs):
    count, width = query.shape
    heads = width // HD
    block = min(512, count)
    scale = HD ** (-0.5)
    query_blocks = query.reshape(count // block, block, heads, HD)
    doc_blocks = docs.reshape(count // block, block)
    key_heads = keys.reshape(count, heads, HD)
    value_heads = values.reshape(count, heads, HD)

    def one_block(inputs):
        query_part, doc_part = inputs
        scores = (
            jnp.einsum("qhd,khd->hqk", query_part, key_heads, preferred_element_type=jnp.float32)
            * scale
        )
        scores = jnp.where((doc_part[:, None] == docs[None, :])[None], scores, MASKED)
        highest = jnp.max(scores, axis=-1, keepdims=True)
        logsum = highest + jnp.log(jnp.sum(jnp.exp(scores - highest), axis=-1, keepdims=True))
        probs = jnp.exp(scores - logsum).astype(jnp.bfloat16)
        mixed = jnp.einsum("hqk,khd->qhd", probs, value_heads, preferred_element_type=jnp.float32)
        return (mixed.reshape(block, width), logsum)

    mixed, logsums = lax.map(one_block, (query_blocks, doc_blocks))
    return (mixed.reshape(count, width), logsums)


def attend_back(query, keys, values, grad_out, logsums, docs):
    count, width = query.shape
    heads = width // HD
    block = min(512, count)
    scale = HD ** (-0.5)
    query_blocks = query.reshape(count // block, block, heads, HD)
    grad_blocks = grad_out.reshape(count // block, block, heads, HD)
    doc_blocks = docs.reshape(count // block, block)
    key_heads = keys.reshape(count, heads, HD)
    value_heads = values.reshape(count, heads, HD)

    def one_block(carry, inputs):
        key_grad, value_grad = carry
        query_part, grad_part, logsum, doc_part = inputs
        scores = (
            jnp.einsum("qhd,khd->hqk", query_part, key_heads, preferred_element_type=jnp.float32)
            * scale
        )
        scores = jnp.where((doc_part[:, None] == docs[None, :])[None], scores, MASKED)
        probs = jnp.exp(scores - logsum)
        prob_low = probs.astype(jnp.bfloat16)
        prob_grad = jnp.einsum(
            "qhd,khd->hqk", grad_part, value_heads, preferred_element_type=jnp.float32
        )
        inner = jnp.sum(probs * prob_grad, axis=-1, keepdims=True)
        score_grad = (probs * (prob_grad - inner)).astype(jnp.bfloat16)
        query_grad = (
            jnp.einsum("hqk,khd->qhd", score_grad, key_heads, preferred_element_type=jnp.float32)
            * scale
        )
        key_grad = (
            key_grad
            + jnp.einsum("hqk,qhd->khd", score_grad, query_part, preferred_element_type=jnp.float32)
            * scale
        )
        value_grad = value_grad + jnp.einsum(
            "hqk,qhd->khd", prob_low, grad_part, preferred_element_type=jnp.float32
        )
        return ((key_grad, value_grad), query_grad.reshape(block, width))

    zeros = jnp.zeros((count, heads, HD), jnp.float32)
    (key_grad, value_grad), query_grad = lax.scan(
        one_block, (zeros, zeros), (query_blocks, grad_blocks, logsums, doc_blocks)
    )
    return (
        query_grad.reshape(count, width),
        key_grad.reshape(count, width),
        value_grad.reshape(count, width),
    )


def expand(low_rows, weight, bias):
    whole = lax.all_gather(low_rows, "mp", axis=0, tiled=True)
    return (whole, jnp.dot(whole, weight, preferred_element_type=jnp.float32) + bias)


def weight_grad(whole, grad_low):
    return contract_rows(whole, grad_low)


def reduce_rows(acts_low, weight):
    return lax.psum_scatter(
        jnp.dot(acts_low, weight, preferred_element_type=jnp.float32),
        "mp",
        scatter_dimension=0,
        tiled=True,
    )


def input_grad(grad_low, weight):
    return lax.psum_scatter(contract_cols(grad_low, weight), "mp", scatter_dimension=0, tiled=True)


def spread_grad(grad_low, acts_low, weight):
    piece = lax.all_gather(grad_low, "mp", axis=0, tiled=True)
    weight_sum = contract_rows(acts_low, piece)
    act_grad = contract_cols(piece, weight)
    return (weight_sum, act_grad)


def layer_forward(resid, params, docs):
    w_proj, w_back, w_up, w_down, b_proj, b_up, gains, shift_rows = params
    width = w_back.shape[0]
    low_in = resid.astype(jnp.bfloat16)
    whole_in, projected = expand(low_in, w_proj, b_proj)
    projected = projected.astype(jnp.bfloat16)
    query = projected[:, :width]
    keys = projected[:, width : 2 * width]
    values = projected[:, 2 * width :]
    attended, logsums = attend(query, keys, values, docs)
    attended = attended.astype(jnp.bfloat16)
    mixed_one = reduce_rows(attended, w_back) + shift_rows[0] + resid
    hidden, normed_one, inverse_one = norm_forward(mixed_one, gains[0], shift_rows[1])
    low_hidden = hidden.astype(jnp.bfloat16)
    whole_hidden, upper = expand(low_hidden, w_up, b_up)
    activated = gelu_value(upper).astype(jnp.bfloat16)
    mixed_two = reduce_rows(activated, w_down) + shift_rows[2] + hidden
    output, normed_two, inverse_two = norm_forward(mixed_two, gains[1], shift_rows[3])
    saved = (
        low_in,
        whole_in,
        query,
        keys,
        values,
        attended,
        logsums,
        normed_one,
        inverse_one,
        low_hidden,
        whole_hidden,
        upper,
        activated,
        normed_two,
        inverse_two,
    )
    return (output, saved)


def layer_backward(grad_out, saved, params, docs, share):
    (
        low_in,
        whole_in,
        query,
        keys,
        values,
        attended,
        logsums,
        normed_one,
        inverse_one,
        low_hidden,
        whole_hidden,
        upper,
        activated,
        normed_two,
        inverse_two,
    ) = saved
    w_proj, w_back, w_up, w_down, b_proj, b_up, gains, shift_rows = params
    width = w_back.shape[0]
    mixed_two_grad, gain_two, shift_two = norm_backward(grad_out, normed_two, inverse_two, gains[1])
    down_grad, act_grad = spread_grad(mixed_two_grad.astype(jnp.bfloat16), activated, w_down)
    upper_grad = (act_grad * gelu_slope(upper)).astype(jnp.bfloat16)
    up_grad = weight_grad(whole_hidden, upper_grad)
    hidden_grad = input_grad(upper_grad, w_up) + mixed_two_grad
    mixed_one_grad, gain_one, shift_one = norm_backward(
        hidden_grad, normed_one, inverse_one, gains[0]
    )
    back_grad, attended_grad = spread_grad(mixed_one_grad.astype(jnp.bfloat16), attended, w_back)
    query_grad, key_grad, value_grad = attend_back(
        query, keys, values, attended_grad.astype(jnp.bfloat16), logsums, docs
    )
    proj_low = jnp.concatenate([query_grad, key_grad, value_grad], axis=1).astype(jnp.bfloat16)
    proj_grad = weight_grad(whole_in, proj_low)
    resid_grad = input_grad(proj_low, w_proj) + mixed_one_grad
    bias_sums = jnp.sum(proj_low.astype(jnp.float32), axis=0)
    grads = (
        jnp.stack(
            [proj_grad[:, :width], proj_grad[:, width : 2 * width], proj_grad[:, 2 * width :]]
        ),
        back_grad,
        up_grad,
        down_grad,
        jnp.stack([bias_sums[:width], bias_sums[2 * width :]]),
        jnp.sum(upper_grad.astype(jnp.float32), axis=0),
        jnp.stack([gain_one, gain_two]) * share,
        jnp.stack(
            [jnp.sum(mixed_one_grad, axis=0), shift_one, jnp.sum(mixed_two_grad, axis=0), shift_two]
        )
        * share,
    )
    return (grads, resid_grad)


def layer_params(layer_index, gathered, b_qv, b_in, ln_gain, shifts):
    proj, back, upward, down = gathered
    width = back.shape[1]
    w_proj = jnp.concatenate(
        [proj[layer_index, 0], proj[layer_index, 1], proj[layer_index, 2]], axis=1
    )
    b_proj = jnp.concatenate(
        [b_qv[layer_index, 0], jnp.zeros((width,), jnp.float32), b_qv[layer_index, 1]]
    )
    return (
        w_proj,
        back[layer_index],
        upward[layer_index],
        down[layer_index],
        b_proj,
        b_in[layer_index],
        ln_gain[layer_index],
        shifts[layer_index],
    )


def sum_bucket_first(parts):
    return lax.psum((parts[0], parts[1], parts[2], parts[3], parts[4], parts[5]), "dp")


def sum_bucket_second(parts):
    return lax.psum((parts[0], parts[1], parts[2], parts[3]), "dp")


def compress(totals, starts, extras, sum_first, sum_second, replicas):
    firsts = tuple(
        (
            jnp.einsum("...mn,...nr->...mr", totals[member], starts[member], precision=HIGHEST)
            for member in range(4)
        )
    )
    summed = sum_first((firsts[0], firsts[1], firsts[2], firsts[3], extras[0], extras[1]))
    bases = tuple((orthogonal(summed[member]) for member in range(4)))
    seconds = tuple(
        (
            jnp.einsum("...mn,...mr->...nr", totals[member], bases[member], precision=HIGHEST)
            for member in range(4)
        )
    )
    second_sums = sum_second((seconds[0], seconds[1], seconds[2], seconds[3]))
    approx = tuple(
        (
            jnp.einsum("...mr,...nr->...mn", bases[member], second_sums[member], precision=HIGHEST)
            / replicas
            for member in range(4)
        )
    )
    return (bases, tuple(second_sums), approx, totals, (summed[4], summed[5]))


def per_device(
    x_in,
    out_grad,
    doc_lengths,
    keep_layer,
    w_qkv,
    w_o,
    w_in,
    w_out,
    b_qv,
    b_in,
    ln_gain,
    shifts,
    m_qkv,
    m_o,
    m_in,
    m_out,
    m_qv,
    m_bin,
    m_gain,
    m_shift,
    e_qkv,
    e_o,
    e_in,
    e_out,
    q_qkv,
    q_o,
    q_in,
    q_out,
):
    gathered = (
        lax.all_gather(w_qkv.astype(jnp.bfloat16), "dp", axis=2, tiled=True),
        lax.all_gather(w_o.astype(jnp.bfloat16), "dp", axis=2, tiled=True),
        lax.all_gather(w_in.astype(jnp.bfloat16), "dp", axis=1, tiled=True),
        lax.all_gather(w_out.astype(jnp.bfloat16), "dp", axis=2, tiled=True),
    )
    own_rows = x_in.shape[0]
    groups = lax.axis_size("mp")
    count = own_rows * groups
    docs = doc_positions(doc_lengths[0], count)
    layer_one = layer_params(0, gathered, b_qv, b_in, ln_gain, shifts)
    layer_two = layer_params(1, gathered, b_qv, b_in, ln_gain, shifts)
    rows_in, grad_rows_in = (x_in, out_grad)
    share = 1.0
    resid = rows_in.astype(jnp.float32)
    first, saved_one = layer_forward(resid, layer_one, docs)
    second, saved_two = layer_forward(first, layer_two, docs)
    keep = keep_layer[0] > 0
    output = jnp.where(keep, second, first)
    grad = grad_rows_in.astype(jnp.float32)
    grads_two, back_two = layer_backward(
        jnp.where(keep, grad, 0.0), saved_two, layer_two, docs, share
    )
    errors = (e_qkv, e_o, e_in, e_out)
    starts = (q_qkv, q_o, q_in, q_out)
    replicas = lax.axis_size("dp")
    grads_one, back_one = layer_backward(
        jnp.where(keep, back_two, grad), saved_one, layer_one, docs, share
    )
    totals = tuple(
        (
            jnp.stack([grads_one[member], grads_two[member]]) + errors[member][0]
            for member in range(4)
        )
    )
    extras = (jnp.stack([grads_one[4], grads_two[4]]), jnp.stack([grads_one[5], grads_two[5]]))
    bases, second_sums, approx, totals, extras = compress(
        totals, starts, extras, sum_bucket_first, sum_bucket_second, replicas
    )
    gain_sum, shift_sum = lax.psum(
        (jnp.stack([grads_one[6], grads_two[6]]), jnp.stack([grads_one[7], grads_two[7]])),
        ("dp", "mp"),
    )
    index = lax.axis_index("dp")

    def renew(weight, moment, approx_full, axis):
        rows = weight.shape[axis]
        part = lax.dynamic_slice_in_dim(approx_full, index * rows, rows, axis)
        moment_new = MOMENTUM * moment + part
        return (weight - RATE * moment_new, moment_new)

    new_w_qkv, new_m_qkv = renew(w_qkv, m_qkv, approx[0], 2)
    new_w_o, new_m_o = renew(w_o, m_o, approx[1], 2)
    new_w_in, new_m_in = renew(w_in, m_in, approx[2], 1)
    new_w_out, new_m_out = renew(w_out, m_out, approx[3], 2)
    new_m_qv = MOMENTUM * m_qv + extras[0] / replicas
    new_m_bin = MOMENTUM * m_bin + extras[1] / replicas
    new_m_gain = MOMENTUM * m_gain + gain_sum / replicas
    new_m_shift = MOMENTUM * m_shift + shift_sum / replicas
    new_errors = tuple(((totals[member] - approx[member])[None] for member in range(4)))
    return (
        output,
        back_one,
        new_w_qkv,
        new_w_o,
        new_w_in,
        new_w_out,
        b_qv - RATE * new_m_qv,
        b_in - RATE * new_m_bin,
        ln_gain - RATE * new_m_gain,
        shifts - RATE * new_m_shift,
        new_m_qkv,
        new_m_o,
        new_m_in,
        new_m_out,
        new_m_qv,
        new_m_bin,
        new_m_gain,
        new_m_shift,
        new_errors[0],
        new_errors[1],
        new_errors[2],
        new_errors[3],
        bases[0],
        bases[1],
        bases[2],
        bases[3],
        second_sums[0],
        second_sums[1],
        second_sums[2],
        second_sums[3],
    )


def solution(mesh):
    in_specs = (
        P(("dp", "mp"), None),
        P(("dp", "mp"), None),
        P("dp", None),
        P("dp"),
        P(None, None, "dp", "mp"),
        P(None, "mp", "dp"),
        P(None, "dp", "mp"),
        P(None, "mp", "dp"),
        P(None, None, "mp"),
        P(None, "mp"),
        P(),
        P(),
        P(None, None, "dp", "mp"),
        P(None, "mp", "dp"),
        P(None, "dp", "mp"),
        P(None, "mp", "dp"),
        P(None, None, "mp"),
        P(None, "mp"),
        P(),
        P(),
        P("dp", None, None, None, "mp"),
        P("dp", None, "mp", None),
        P("dp", None, None, "mp"),
        P("dp", None, "mp", None),
        P(None, None, "mp", None),
        P(None, "mp", None),
        P(None, "mp", None),
        P(None, "mp", None),
    )
    out_specs = (
        P(("dp", "mp"), None),
        P(("dp", "mp"), None),
        P(None, None, "dp", "mp"),
        P(None, "mp", "dp"),
        P(None, "dp", "mp"),
        P(None, "mp", "dp"),
        P(None, None, "mp"),
        P(None, "mp"),
        P(),
        P(),
        P(None, None, "dp", "mp"),
        P(None, "mp", "dp"),
        P(None, "dp", "mp"),
        P(None, "mp", "dp"),
        P(None, None, "mp"),
        P(None, "mp"),
        P(),
        P(),
        P("dp", None, None, None, "mp"),
        P("dp", None, "mp", None),
        P("dp", None, None, "mp"),
        P("dp", None, "mp", None),
        P(None, None, "mp", None),
        P(None, "mp", None),
        P(None, "mp", None),
        P(None, "mp", None),
        P(None, None, "mp", None),
        P(None, "mp", None),
        P(None, "mp", None),
        P(None, "mp", None),
    )
    return jax.shard_map(
        per_device, mesh=mesh, in_specs=in_specs, out_specs=out_specs, check_vma=False
    )
```

profile of v0, /device:TPU:0, one launch (start us, length us, event | category | flops | bytes accessed | tf_op | source)
XLA Modules:
  0.0 1085.7 jit_solution(4361939193061036483)
XLA Ops:
  11.9 35.0 %all_gather.38 = bf16[2,192,768]{1,0,2:T(2,128)(2,1)S(1)} all-gather(bf16[2,192,96]{1,0,2:T(2,128)(2,1)S(1)} %copy.172), channel_id=1, replica_groups=mesh['dp'=8,'mp'=4] {'dp'}, dimensions={2}, use_global_device_ids=true | all-gather | bytes 663552 | tf_op jit(solution)/shard_map/all_gather | solution.py:359
  49.2 19.4 %all-gather.12.cloned.1.call-done = bf16[2,3,768,192]{3,2,1,0:T(8,128)(2,1)} async-done(((bf16[2,3,96,192]{3,2,1,0:T(8,128)(2,1)}), bf16[2,3,768,192]{3,2,1,0:T(8,128)(2,1)}) %all-gather.12.cloned.1.call-update) | async-done | bytes 1769488 | tf_op jit(solution)/shard_map/all_gather | solution.py:358
  71.3 17.7 %all-gather.14.cloned.1.call-done = bf16[1024,768]{1,0:T(8,128)(2,1)} async-done(((bf16[256,768]{1,0:T(8,128)(2,1)}), bf16[1024,768]{1,0:T(8,128)(2,1)}) %all-gather.14.cloned.1.call-update) | async-done | bytes 1572880 | tf_op jit(solution)/shard_map/all_gather | solution.py:152
  92.3 11.2 %while.54 = (s32[]{:T(128)}, bf16[2,512,192]{1,2,0:T(8,128)(2,1)S(1)}, f32[2,3,512,1]{2,1,3,0:T(4,128)S(1)}, s32[2,512]{1,0:T(2,128)S(1)}, s32[1024]{0:T(1024)S(...) while((s32[]{:T(128)}, ...), condition=%wide.region_5.6_spmd, body=%wide.region_2.5_spmd.sunk | while | flops 420477440 | bytes 22612076 | solution.py:96
  109.4 35.6 %reduce-scatter.9.cloned.1.call-done = f32[256,768]{1,0:T(8,128)} async-done(((f32[1024,768]{1,0:T(8,128)}), f32[256,768]{1,0:T(8,128)}) %reduce-scatter.9.cloned.1.call-update) | async-done | bytes 786448 | tf_op jit(solution)/shard_map/reduce_scatter | solution.py:161
  149.0 50.9 %all-gather.18.cloned.1.call-done = bf16[2,768,768]{2,1,0:T(8,128)(2,1)} async-done(((bf16[2,96,768]{2,1,0:T(8,128)(2,1)}), bf16[2,768,768]{2,1,0:T(8,128)(2,1)}) %all-gather.18.cloned.1.call-update) | async-done | bytes 2359312 | tf_op jit(solution)/shard_map/all_gather | solution.py:360
  199.9 20.3 %all-gather.16.cloned.1.call-done = bf16[1024,768]{1,0:T(8,128)(2,1)} async-done(((bf16[256,768]{1,0:T(8,128)(2,1)}), bf16[1024,768]{1,0:T(8,128)(2,1)}) %all-gather.16.cloned.1.call-update) | async-done | bytes 1572880 | tf_op jit(solution)/shard_map/all_gather | solution.py:152
  220.2 5.4 multiply_convert_fusion.3
  225.6 49.6 %all-gather.20.cloned.1.call-done = bf16[2,768,768]{1,2,0:T(8,128)(2,1)} async-done(((bf16[2,768,96]{1,2,0:T(8,128)(2,1)}), bf16[2,768,768]{1,2,0:T(8,128)(2,1)}) %all-gather.20.cloned.1.call-update) | async-done | bytes 2359312 | tf_op jit(solution)/shard_map/all_gather | solution.py:361
  275.2 4.8 fusion.89
  280.2 36.4 %reduce-scatter.11.cloned.1.call-done = f32[256,768]{1,0:T(8,128)} async-done(((f32[1024,768]{1,0:T(8,128)}), f32[256,768]{1,0:T(8,128)}) %reduce-scatter.11.cloned.1.call-update) | async-done | bytes 786448 | tf_op jit(solution)/shard_map/reduce_scatter | solution.py:161
  319.9 19.3 %all-gather.22.cloned.1.call-done = bf16[1024,768]{1,0:T(8,128)(2,1)} async-done(((bf16[256,768]{1,0:T(8,128)(2,1)}), bf16[1024,768]{1,0:T(8,128)(2,1)}) %all-gather.22.cloned.1.call-update) | async-done | bytes 1572880 | tf_op jit(solution)/shard_map/all_gather | solution.py:152
  342.5 11.2 %while.55 = (s32[]{:T(128)}, bf16[2,512,192]{1,2,0:T(8,128)(2,1)S(1)}, f32[2,3,512,1]{2,1,3,0:T(4,128)S(1)}, s32[2,512]{1,0:T(2,128)S(1)}, s32[1024]{0:T(1024)S(...) while((s32[]{:T(128)}, ...), condition=%wide.region_15.16_spmd, body=%wide.region_12.15_spmd.sunk | while | flops 420477440 | bytes 22612076 | solution.py:96
  356.2 38.0 %reduce-scatter.13.cloned.1.call-done = f32[256,768]{1,0:T(8,128)} async-done(((f32[1024,768]{1,0:T(8,128)}), f32[256,768]{1,0:T(8,128)}) %reduce-scatter.13.cloned.1.call-update) | async-done | bytes 786448 | tf_op jit(solution)/shard_map/reduce_scatter | solution.py:161
  397.0 19.8 %all-gather.24.cloned.1.call-done = bf16[1024,768]{1,0:T(8,128)(2,1)} async-done(((bf16[256,768]{1,0:T(8,128)(2,1)}), bf16[1024,768]{1,0:T(8,128)(2,1)}) %all-gather.24.cloned.1.call-update) | async-done | bytes 1572880 | tf_op jit(solution)/shard_map/all_gather | solution.py:152
  416.8 5.0 multiply_convert_fusion.2
  426.9 37.4 %reduce-scatter.15.cloned.1.call-done = f32[256,768]{1,0:T(8,128)} async-done(((f32[1024,768]{1,0:T(8,128)}), f32[256,768]{1,0:T(8,128)}) %reduce-scatter.15.cloned.1.call-update) | async-done | bytes 786448 | tf_op jit(solution)/shard_map/reduce_scatter | solution.py:161
  468.7 19.8 %all-gather.26.cloned.1.call-done = bf16[1024,768]{1,0:T(8,128)(2,1)} async-done(((bf16[256,768]{1,0:T(8,128)(2,1)}), bf16[1024,768]{1,0:T(8,128)(2,1)}) %all-gather.26.cloned.1.call-update) | async-done | bytes 1572880 | tf_op jit(solution)/shard_map/all_gather | solution.py:174
  488.5 5.5 convert_reduce_fusion
  495.1 3.1 fusion.90
  498.3 38.1 %reduce-scatter.17.cloned.1.call-done = f32[256,768]{1,0:T(8,128)} async-done(((f32[1024,768]{1,0:T(8,128)}), f32[256,768]{1,0:T(8,128)}) %reduce-scatter.17.cloned.1.call-update) | async-done | bytes 786448 | tf_op jit(solution)/shard_map/reduce_scatter | solution.py:170
  540.6 19.5 %all-gather.28.cloned.1.call-done = bf16[1024,768]{1,0:T(8,128)(2,1)} async-done(((bf16[256,768]{1,0:T(8,128)(2,1)}), bf16[1024,768]{1,0:T(8,128)(2,1)}) %all-gather.28.cloned.1.call-update) | async-done | bytes 1572880 | tf_op jit(solution)/shard_map/all_gather | solution.py:174
  563.3 31.4 %while.56 = (s32[]{:T(128)}, f32[1024,3,64]{0,2,1:T(8,128)}, f32[1024,3,64]{0,2,1:T(8,128)}, bf16[2,512,192]{1,2,0:T(8,128)(2,1)}, bf16[2,512,3,64]{1,3,2,0:T(8,...) while((s32[]{:T(128)}, f32[1024,3,64]{0,2,1:T(8,128)}, ...), condition=%wide.region_29.30_spmd.clone, body=%wide.region_27.29_spmd.clone.sunk | while | flops 1031928320 | bytes 125296200 | solution.py:141
  574.8 3.9 fusion.253
  590.5 4.2 fusion.253
  599.4 3.3 fusion.106
  602.8 38.0 %reduce-scatter.19.cloned.1.call-done = f32[256,768]{1,0:T(8,128)} async-done(((f32[1024,768]{1,0:T(8,128)}), f32[256,768]{1,0:T(8,128)}) %reduce-scatter.19.cloned.1.call-update) | async-done | bytes 786448 | tf_op jit(solution)/shard_map/reduce_scatter | solution.py:170
  647.4 19.4 %all-gather.30.cloned.1.call-done = bf16[1024,768]{1,0:T(8,128)(2,1)} async-done(((bf16[256,768]{1,0:T(8,128)(2,1)}), bf16[1024,768]{1,0:T(8,128)(2,1)}) %all-gather.30.cloned.1.call-update) | async-done | bytes 1572880 | tf_op jit(solution)/shard_map/all_gather | solution.py:174
  666.8 4.9 convert_reduce_fusion.1
  685.2 28.9 %reduce-scatter.21.cloned.1.call-done = f32[256,768]{1,0:T(8,128)} async-done(((f32[1024,768]{1,0:T(8,128)}), f32[256,768]{1,0:T(8,128)}) %reduce-scatter.21.cloned.1.call-update) | async-done | bytes 786448 | tf_op jit(solution)/shard_map/reduce_scatter | solution.py:170
  727.2 4.8 fusion.126
  734.9 4.9 fusion.128
  743.0 33.6 %while.57 = (s32[]{:T(128)}, f32[1024,3,64]{0,2,1:T(8,128)}, f32[1024,3,64]{0,2,1:T(8,128)}, bf16[2,512,192]{1,2,0:T(8,128)(2,1)}, bf16[2,512,3,64]{1,3,2,0:T(8,...) while((s32[]{:T(128)}, f32[1024,3,64]{0,2,1:T(8,128)}, ...), condition=%wide.region_38.39_spmd.clone, body=%wide.region_36.38_spmd.clone.sunk | while | flops 1031928320 | bytes 119005144 | solution.py:141
  755.7 3.9 fusion.265
  772.4 4.2 fusion.265
  793.4 63.1 %all-reduce.11.cloned.1.call-done = (f32[2,192,8]{1,2,0:T(8,128)}, f32[2,768,8]{1,2,0:T(8,128)}, f32[2,768,8]{1,2,0:T(8,128)}) async-done(((f32[2,192,8]{1,2,0:T(8,128)}, f32[2,768,8]{1,2,0:T(8,128)}, f32[2,768,8]{1,2,0:T(8,128)}), (f32[2,192,8]{1,2,0:T(8,128)}, f32[2,768,8]{1,2,0:T(8,128)}, f32[2,768,8]{1,2,0:T(8,128)})) %all-reduce.11.cloned.1.call-update) | async-done | bytes 110608 | tf_op jit(solution)/shard_map/psum | solution.py:294
  862.7 7.1 fusion.125
  872.7 7.0 fusion.127
  885.2 45.2 %all-reduce.7.cloned.1.call-done = f32[2,3,768,8]{2,3,1,0:T(8,128)} async-done(((f32[2,3,768,8]{2,3,1,0:T(8,128)}), f32[2,3,768,8]{2,3,1,0:T(8,128)}) %all-reduce.7.cloned.1.call-update) | async-done | bytes 147472 | tf_op jit(solution)/shard_map/psum | solution.py:294
  942.9 6.5 fusion.123
  949.5 4.8 fusion.107
  963.6 40.1 %all-reduce = (f32[2,2,768]{2,1,0:T(2,128)S(1)}, f32[2,4,768]{2,1,0:T(4,128)S(1)}) all-reduce(f32[2,2,768]{2,1,0:T(2,128)S(1)} %pad_maximum_fusion.9, f32[2,4,768]{2,1,0:T(4,128)S(1)} %pad_maximum_fusion.8), channel_id=1, replica_groups=mesh['dp'=8,'mp'=4] {'dp','mp'}, use_global_device_ids=true, to_apply=%region_118.119 | all-reduce | flops 9216 | bytes 73728 | tf_op jit(solution)/shard_map/psum | solution.py:396
  1004.9 15.0 %all-reduce.9.cloned.1.call-done = (f32[2,3,192,8]{2,3,1,0:T(8,128)}, f32[2,768,8]{1,2,0:T(8,128)}, f32[2,768,8]{1,2,0:T(8,128)}, f32[2,768,8]{1,2,0:T(8,128)}, f32[2,2,192]{2,1,0:T(2,128)}, /*index=5*/f32[2,768]{1,0:T(2,128)}) async-done(((f32[2,3,192,8]{2,3,1,0:T(8,128)}, f32[2,768,8]{1,2,0:T(8,128)}, f32[2,768,8]{1,2,0:T(8,128)}, f32[2,768,8]{1,2,0:T(8,128)}, f32[2,2,192]{2,1,0:T(2,128)}, ...) | async-done | bytes 193552 | tf_op jit(solution)/shard_map/psum | solution.py:298
  1020.0 4.9 broadcast_multiply_fusion
  1047.8 4.2 broadcast_multiply_fusion.1
  1057.9 4.7 subtract_bitcast_fusion.2
  1062.7 5.6 subtract_bitcast_fusion
  1068.4 5.5 subtract_bitcast_fusion.1
  (864 shorter events, 252.6 us)
Async XLA Ops:
  7.2 782.4 %copy-start = (f32[2,3,192,8]{2,3,1,0:T(8,128)S(1)}, f32[2,3,192,8]{2,3,1,0:T(8,128)}, u32[]{:S(2)}) copy-start(f32[2,3,192,8]{2,3,1,0:T(8,128)} %param.60) | copy-start | bytes 110596
  7.2 61.4 %all-gather.12.cloned.1.call-start = ((), (), s32[]{:S(2)}) async-start(), calls=%async_computation.8 | async-start | bytes 2654208 | tf_op jit(solution)/shard_map/all_gather | solution.py:358
  9.1 79.8 %all-gather.14.cloned.1.call-start = ((), (), s32[]{:S(2)}) async-start(), calls=%async_computation.9 | async-start | bytes 1966080 | tf_op jit(solution)/shard_map/all_gather | solution.py:152
  9.9 135.1 %reduce-scatter.9.cloned.1.call-start = ((), (), s32[]{:S(2)}) async-start(), calls=%async_computation.10 | async-start | bytes 3932160 | tf_op jit(solution)/shard_map/reduce_scatter | solution.py:161
  11.9 36.6 %copy-start.138 = (f32[2,2,192]{2,1,0:T(2,128)S(1)}, f32[2,2,192]{2,1,0:T(2,128)}, u32[]{:S(2)}) copy-start(f32[2,2,192]{2,1,0:T(2,128)} %param.44) | copy-start | bytes 9220
  48.5 55.1 %copy-start.82 = (bf16[1,192,768]{2,1,0:T(8,128)(2,1)}, bf16[1,192,768]{2,1,0:T(8,128)(2,1)S(1)}, u32[]{:S(2)}) copy-start(bf16[1,192,768]{2,1,0:T(8,128)(2,1)S(1)} %copy.223) | copy-start | bytes 884740
  106.8 38.1 %copy-start.68 = (bf16[256,768]{1,0:T(8,128)(2,1)S(1)}, bf16[256,768]{1,0:T(8,128)(2,1)}, u32[]{:S(2)}) copy-start(bf16[256,768]{1,0:T(8,128)(2,1)} %param.36) | copy-start | bytes 1179652
  106.8 93.1 %all-gather.18.cloned.1.call-start = ((), (), s32[]{:S(2)}) async-start(), calls=%async_computation.12 | async-start | bytes 2654208 | tf_op jit(solution)/shard_map/all_gather | solution.py:360
  108.6 39.0 %copy-start.61 = (f32[2,768,96]{1,2,0:T(8,128)S(1)}, f32[2,768,96]{1,2,0:T(8,128)}, u32[]{:S(2)}) copy-start(f32[2,768,96]{1,2,0:T(8,128)} %param.43) | copy-start | bytes 1769476
  108.6 111.6 %all-gather.16.cloned.1.call-start = ((), (), s32[]{:S(2)}) async-start(), calls=%async_computation.11 | async-start | bytes 1966080 | tf_op jit(solution)/shard_map/all_gather | solution.py:152
  108.7 207.9 %copy-start.112 = (f32[768]{0:T(1024)}, f32[768]{0:T(1024)S(1)}, u32[]{:S(2)}) copy-start(f32[768]{0:T(1024)S(1)} %get-tuple-element.683) | copy-start | bytes 9220
  146.3 170.4 %copy-start.22 = (f32[256,768]{1,0:T(8,128)}, f32[256,768]{1,0:T(8,128)S(1)}, u32[]{:S(2)}) copy-start(f32[256,768]{1,0:T(8,128)S(1)} %get-tuple-element.827) | copy-start | bytes 2359300
  146.3 170.4 %copy-start.122 = (f32[256]{0:T(256)}, f32[256]{0:T(256)S(1)}, u32[]{:S(2)}) copy-start(f32[256]{0:T(256)S(1)} %broadcast_multiply_fusion.17) | copy-start | bytes 3076
  146.5 170.1 %copy-start.124 = (f32[256]{0:T(256)}, f32[256]{0:T(256)S(1)}, u32[]{:S(2)}) copy-start(f32[256]{0:T(256)S(1)} %add_rsqrt_fusion.11) | copy-start | bytes 3076
  147.5 127.7 %all-gather.20.cloned.1.call-start = ((), (), s32[]{:S(2)}) async-start(), calls=%async_computation.13 | async-start | bytes 2654208 | tf_op jit(solution)/shard_map/all_gather | solution.py:361
  148.3 168.3 %reduce-scatter.11.cloned.1.call-start = ((), (), s32[]{:S(2)}) async-start(), calls=%async_computation.14 | async-start | bytes 3932160 | tf_op jit(solution)/shard_map/reduce_scatter | solution.py:161
  149.0 76.6 %copy-start.148 = (f32[768]{0:T(1024)}, f32[768]{0:T(1024)S(1)}, u32[]{:S(2)}) copy-start(f32[768]{0:T(1024)S(1)} %get-tuple-element.685) | copy-start | bytes 9220
  280.0 59.2 %all-gather.22.cloned.1.call-start = ((), (), s32[]{:S(2)}) async-start(), calls=%async_computation.15 | async-start | bytes 1966080 | tf_op jit(solution)/shard_map/all_gather | solution.py:152
  318.1 76.1 %copy-start.24 = (f32[256,768]{1,0:T(8,128)}, f32[256,768]{1,0:T(8,128)S(1)}, u32[]{:S(2)}) copy-start(f32[256,768]{1,0:T(8,128)S(1)} %get-tuple-element.825) | copy-start | bytes 2359300
  319.4 74.9 %reduce-scatter.13.cloned.1.call-start = ((), (), s32[]{:S(2)}) async-start(), calls=%async_computation.16 | async-start | bytes 3932160 | tf_op jit(solution)/shard_map/reduce_scatter | solution.py:161
  356.2 60.6 %all-gather.24.cloned.1.call-start = ((), (), s32[]{:S(2)}) async-start(), calls=%async_computation.17 | async-start | bytes 1966080 | tf_op jit(solution)/shard_map/all_gather | solution.py:152
  396.9 67.3 %reduce-scatter.15.cloned.1.call-start = ((), (), s32[]{:S(2)}) async-start(), calls=%async_computation.18 | async-start | bytes 3932160 | tf_op jit(solution)/shard_map/reduce_scatter | solution.py:161
  426.1 39.8 %copy-start.57 = (bf16[256,768]{1,0:T(8,128)(2,1)S(1)}, bf16[256,768]{1,0:T(8,128)(2,1)}, u32[]{:S(2)}) copy-start(bf16[256,768]{1,0:T(8,128)(2,1)} %param.37) | copy-start | bytes 1179652
  426.2 62.3 %all-gather.26.cloned.1.call-start = ((), (), s32[]{:S(2)}) async-start(), calls=%async_computation.19 | async-start | bytes 1966080 | tf_op jit(solution)/shard_map/all_gather | solution.py:174
  468.6 67.7 %reduce-scatter.17.cloned.1.call-start = ((), (), s32[]{:S(2)}) async-start(), calls=%async_computation.20 | async-start | bytes 3932160 | tf_op jit(solution)/shard_map/reduce_scatter | solution.py:170
  498.3 61.9 %all-gather.28.cloned.1.call-start = ((), (), s32[]{:S(2)}) async-start(), calls=%async_computation.21 | async-start | bytes 1966080 | tf_op jit(solution)/shard_map/all_gather | solution.py:174
  540.3 100.5 %reduce-scatter.19.cloned.1.call-start = ((), (), s32[]{:S(2)}) async-start(), calls=%async_computation.22 | async-start | bytes 3932160 | tf_op jit(solution)/shard_map/reduce_scatter | solution.py:170
  602.7 38.1 %copy-start.25 = (f32[256,768]{1,0:T(8,128)S(1)}, f32[256,768]{1,0:T(8,128)}, u32[]{:S(2)}) copy-start(f32[256,768]{1,0:T(8,128)} %copy-done.24) | copy-start | bytes 2359300
  602.7 38.1 %copy-start.47 = (f32[256,768]{1,0:T(8,128)S(1)}, f32[256,768]{1,0:T(8,128)}, u32[]{:S(2)}) copy-start(f32[256,768]{1,0:T(8,128)} %copy-done.46) | copy-start | bytes 2359300
  602.7 38.1 %copy-start.58 = (bf16[256,768]{1,0:T(8,128)(2,1)S(1)}, bf16[256,768]{1,0:T(8,128)(2,1)}, u32[]{:S(2)}) copy-start(bf16[256,768]{1,0:T(8,128)(2,1)} %param.37) | copy-start | bytes 1179652
  602.7 40.3 %copy-start.33 = (f32[256,768]{1,0:T(8,128)S(1)}, f32[256,768]{1,0:T(8,128)}, u32[]{:S(2)}) copy-start(f32[256,768]{1,0:T(8,128)} %copy-done.32) | copy-start | bytes 2359300
  602.7 40.3 %copy-start.140 = (f32[768]{0:T(1024)S(1)}, f32[768]{0:T(1024)}, u32[]{:S(2)}) copy-start(f32[768]{0:T(1024)} %get-tuple-element.672) | copy-start | bytes 9220
  602.7 64.1 %all-gather.30.cloned.1.call-start = ((), (), s32[]{:S(2)}) async-start(), calls=%async_computation.23 | async-start | bytes 1966080 | tf_op jit(solution)/shard_map/all_gather | solution.py:174
  647.0 67.2 %reduce-scatter.21.cloned.1.call-start = ((), (), s32[]{:S(2)}) async-start(), calls=%async_computation.24 | async-start | bytes 3932160 | tf_op jit(solution)/shard_map/reduce_scatter | solution.py:170
  676.0 63.7 %all-gather.32.cloned.1.call-start = ((), (), s32[]{:S(2)}) async-start(), calls=%async_computation.25 | async-start | bytes 1966080 | tf_op jit(solution)/shard_map/all_gather | solution.py:174
  682.4 51.1 %copy-start.28 = (f32[1,768,768]{2,1,0:T(8,128)}, f32[1,768,768]{2,1,0:T(8,128)S(1)}, u32[]{:S(2)}) copy-start(f32[1,768,768]{2,1,0:T(8,128)S(1)} %convolution_bitcast_fusion.2) | copy-start | bytes 7077892
  682.9 31.2 %copy-start.125 = (f32[256]{0:T(256)S(1)}, f32[256]{0:T(256)}, u32[]{:S(2)}) copy-start(f32[256]{0:T(256)} %copy-done.124) | copy-start | bytes 3076
  719.2 137.4 %all-reduce.11.cloned.1.call-start = ((), (), s32[]{:S(2)}) async-start(), calls=%async_computation.29 | async-start | bytes 229376 | tf_op jit(solution)/shard_map/psum | solution.py:294
  786.6 143.8 %all-reduce.7.cloned.1.call-start = ((), (), s32[]{:S(2)}) async-start(), calls=%async_computation.27 | async-start | bytes 294912 | tf_op jit(solution)/shard_map/psum | solution.py:294
  792.9 227.1 %all-reduce.9.cloned.1.call-start = ((), (), s32[]{:S(2)}) async-start(), calls=%async_computation.28 | async-start | bytes 413696 | tf_op jit(solution)/shard_map/psum | solution.py:298
  882.6 162.2 %copy-start.111 = (f32[2,192,8]{1,2,0:T(8,128)}, f32[2,192,8]{1,2,0:T(8,128)S(1)}, u32[]{:S(2)}) copy-start(f32[2,192,8]{1,2,0:T(8,128)S(1)} %concatenate.39) | copy-start | bytes 36868
  942.9 90.2 %copy-start.81 = (f32[2,3,768,8]{2,3,1,0:T(8,128)}, f32[2,3,768,8]{2,3,1,0:T(8,128)S(1)}, u32[]{:S(2)}) copy-start(f32[2,3,768,8]{2,3,1,0:T(8,128)S(1)} %concatenate.38) | copy-start | bytes 442372
  949.5 124.3 %reduce-scatter.23.cloned.1.call-start = ((), (), s32[]{:S(2)}) async-start(), calls=%async_computation.26 | async-start | bytes 3932160 | tf_op jit(solution)/shard_map/reduce_scatter | solution.py:170
  956.7 47.0 %copy-start.120 = (f32[2,2,768]{2,1,0:T(2,128)S(1)}, f32[2,2,768]{2,1,0:T(2,128)}, u32[]{:S(2)}) copy-start(f32[2,2,768]{2,1,0:T(2,128)} %param.46) | copy-start | bytes 36868
  956.7 47.0 %copy-start.144 = (f32[2,2,768]{2,1,0:T(2,128)S(1)}, f32[2,2,768]{2,1,0:T(2,128)}, u32[]{:S(2)}) copy-start(f32[2,2,768]{2,1,0:T(2,128)} %param.54) | copy-start | bytes 36868
  956.7 47.6 %copy-start.115 = (f32[2,4,768]{2,1,0:T(4,128)S(1)}, f32[2,4,768]{2,1,0:T(4,128)}, u32[]{:S(2)}) copy-start(f32[2,4,768]{2,1,0:T(4,128)} %param.47) | copy-start | bytes 73732
  956.7 47.6 %copy-start.128 = (f32[2,4,768]{2,1,0:T(4,128)S(1)}, f32[2,4,768]{2,1,0:T(4,128)}, u32[]{:S(2)}) copy-start(f32[2,4,768]{2,1,0:T(4,128)} %param.55) | copy-start | bytes 73732
  956.7 63.3 %copy-start.87 = (f32[2,768,8]{1,2,0:T(8,128)S(1)}, f32[2,768,8]{1,2,0:T(8,128)}, u32[]{:S(2)}) copy-start(f32[2,768,8]{1,2,0:T(8,128)} %copy-done.86) | copy-start | bytes 147460
  (180 other events, 934.2 us)
Sparse Core Ops, SparseCore 0:
  10.8 57.7 all-gather.11
  70.2 18.6 all-gather.13
  106.9 37.9 reduce-scatter.8
  147.8 52.0 all-gather.17
  202.0 18.1 all-gather.15
  223.0 52.0 all-gather.19
  280.1 36.4 reduce-scatter.10
  319.5 19.6 all-gather.21
  356.3 37.9 reduce-scatter.12
  397.1 19.6 all-gather.23
  426.3 37.9 reduce-scatter.14
  468.8 19.6 all-gather.25
  498.4 37.9 reduce-scatter.16
  540.4 19.6 all-gather.27
  602.8 37.9 reduce-scatter.18
  647.1 19.6 all-gather.29
  676.2 37.9 reduce-scatter.20
  719.3 19.6 all-gather.31
  786.7 69.7 all-reduce.10
  860.3 70.1 all-reduce.6
  949.6 70.3 all-reduce.8
  1022.5 38.0 reduce-scatter.22
where the time goes:
time: 1100 us; the launch traced here: 1090 us
  waiting for transfers between devices  632 us (57%)
  matrix products  186 us (17%)
  other arithmetic  104 us (9%)
  blocking collectives  75.1 us (7%)
  local copies, waits for them, and re-layouts  67.4 us (6%)
  between operations  17.5 us (2%)
    reduce_scatter x4, waiting for transfers between devices, reduce_rows(): lax.psum_scatter(jnp.dot(acts_low, weight, preferred_element_type=jnp.flo...  147 us
    psum x2, waiting for transfers between devices, sum_bucket_first(): lax.psum((parts[0], parts[1], parts[2], parts[3], parts[4], parts[5]), 'dp')  108 us
    reduce_scatter x4, waiting for transfers between devices, input_grad(): lax.psum_scatter(contract_cols(grad_low, weight), 'mp', scatter_dimension...  105 us
    all_gather x4, waiting for transfers between devices, expand(): whole = lax.all_gather(low_rows, 'mp', axis=0, tiled=True)  77 us
    all_gather x4, waiting for transfers between devices, spread_grad(): piece = lax.all_gather(grad_low, 'mp', axis=0, tiled=True)  58.7 us
    all_gather x1, waiting for transfers between devices, per_device(): lax.all_gather(w_in.astype(jnp.bfloat16), 'dp', axis=1, tiled=True)  50.9 us
    all_gather x1, waiting for transfers between devices, per_device(): lax.all_gather(w_out.astype(jnp.bfloat16), 'dp', axis=2, tiled=True)  49.6 us
    unnamed x351, local copies, waits for them, and re-layouts  49.3 us
  transfers between devices with their start and end apart: 22, of which 20 were waited for; matrix products, arithmetic and copies ran while one was open for 13% of the time, Pallas kernels for 0%

commit v1 on v0

v1 whole, which is shorter than its diff:
```python
import jax
import jax.numpy as jnp
from jax import lax
from jax.sharding import PartitionSpec as P

HD = 64


NORM_EPS = 1e-05
ORTHO_EPS = 1e-06
MOMENTUM = 0.9
RATE = 0.05
MASKED = -1000000000.0
ROOT_HALF = 0.7071067811865476
INV_ROOT_TWO_PI = 0.3989422804014327
HIGHEST = lax.Precision.HIGHEST
LOW = jnp.bfloat16
F32 = jnp.float32


def dot(left, right, left_dim, right_dim, precision=None):
    return lax.dot_general(
        left,
        right,
        (((left_dim,), (right_dim,)), ((), ())),
        preferred_element_type=F32,
        precision=precision,
    )


def swap(value, axis, bit):
    size = lax.axis_size(axis)
    return lax.ppermute(value, axis, [(i, i ^ bit) for i in range(size)])


def gelu_parts(upper):
    cdf = 0.5 * (1.0 + lax.erf(upper * ROOT_HALF))
    slope = cdf + upper * jnp.exp(-0.5 * upper * upper) * INV_ROOT_TWO_PI
    return upper * cdf, slope


def norm_forward(rows_in, gain, shift):
    centred = rows_in - jnp.mean(rows_in, axis=-1, keepdims=True)
    inverse = lax.rsqrt(jnp.mean(centred * centred, axis=-1, keepdims=True) + NORM_EPS)
    normed = centred * inverse
    return (normed * gain + shift, normed, inverse)


def norm_backward(grad, normed, inverse, gain):
    scaled = grad * gain
    inner = jnp.mean(scaled * normed, axis=-1, keepdims=True)
    return inverse * (scaled - jnp.mean(scaled, axis=-1, keepdims=True) - normed * inner)


def doc_index(lengths, places):
    slots = jnp.arange(lengths.shape[0])
    ends = jnp.sum(jnp.where(slots[:, None] <= slots[None, :], lengths[:, None], 0), axis=0)
    return jnp.sum((places[:, None] >= ends[None, :]).astype(jnp.int32), axis=1)


def orthogonal_rows(factor):
    rank = factor.shape[-2]
    done = []
    for row in range(rank):
        vector = factor[..., :1, :]
        vector = vector * lax.rsqrt(jnp.sum(vector * vector, axis=-1, keepdims=True) + ORTHO_EPS)
        done.append(vector)
        if row + 1 < rank:
            remain = factor[..., 1:, :]
            factor = remain - vector * jnp.sum(vector * remain, axis=-1, keepdims=True)
    return jnp.concatenate(done, axis=-2)


def attend(query, keys, values, docs):
    count, width = query.shape
    heads = width // HD
    scale = HD ** (-0.5)
    same = docs[:, None] == docs[None, :]
    outs, logsums = [], []
    for head in range(heads):
        cols = slice(head * HD, (head + 1) * HD)
        scores = dot(query[:, cols], keys[:, cols], 1, 1) * scale
        scores = jnp.where(same, scores, MASKED)
        highest = jnp.max(scores, axis=-1, keepdims=True)
        logsum = highest + jnp.log(jnp.sum(jnp.exp(scores - highest), axis=-1, keepdims=True))
        probs = jnp.exp(scores - logsum).astype(LOW)
        outs.append(dot(probs, values[:, cols], 1, 0))
        logsums.append(logsum)
    return jnp.concatenate(outs, axis=1), logsums


def attend_back(query, keys, values, grad_out, logsums, docs):
    count, width = query.shape
    heads = width // HD
    scale = HD ** (-0.5)
    same = docs[:, None] == docs[None, :]
    dq, dk, dv = [], [], []
    for head in range(heads):
        cols = slice(head * HD, (head + 1) * HD)
        scores = dot(query[:, cols], keys[:, cols], 1, 1) * scale
        scores = jnp.where(same, scores, MASKED)
        probs = jnp.exp(scores - logsums[head])
        prob_grad = dot(grad_out[:, cols], values[:, cols], 1, 1)
        inner = jnp.sum(probs * prob_grad, axis=-1, keepdims=True)
        score_grad = (probs * (prob_grad - inner)).astype(LOW)
        dq.append(dot(score_grad, keys[:, cols], 1, 0) * scale)
        dk.append(dot(score_grad, query[:, cols], 0, 0) * scale)
        dv.append(dot(probs.astype(LOW), grad_out[:, cols], 0, 0))
    return jnp.concatenate(dq + dk + dv, axis=1).astype(LOW)


def core_sum(partial):
    half = partial.shape[0] // 2
    arrived = swap(partial[half:].astype(LOW), "mp", 1)
    return partial[:half] + arrived.astype(F32)


def chip_sum(part):
    arrived = swap(part.astype(LOW), "mp", 2).astype(F32)
    half = part.shape[0] // 2
    return part + jnp.concatenate([arrived[half:], arrived[:half]], axis=0)


def group_sum(partial):
    return chip_sum(core_sum(partial))


def core_whole(low_rows):
    return jnp.concatenate([low_rows, swap(low_rows, "mp", 1)], axis=0)


def layer_forward(resid, whole_in, params, docs):
    w_proj, w_back_t, w_up, w_down_t, b_proj, b_up, gains, shift_rows = params
    width = w_back_t.shape[1]
    projected = (dot(whole_in, w_proj, 1, 0) + b_proj).astype(LOW)
    query = projected[:, :width]
    keys = projected[:, width : 2 * width]
    values = projected[:, 2 * width :]
    attended, logsums = attend(query, keys, values, docs)
    attended = attended.astype(LOW)
    mixed_one = group_sum(dot(attended, w_back_t, 1, 1)) + shift_rows[0] + resid
    hidden, normed_one, inverse_one = norm_forward(mixed_one, gains[0], shift_rows[1])
    whole_hidden = core_whole(hidden.astype(LOW))
    upper = dot(whole_hidden, w_up, 1, 0) + b_up
    activated, slope = gelu_parts(upper)
    activated = activated.astype(LOW)
    mixed_two = group_sum(dot(activated, w_down_t, 1, 1)) + shift_rows[2] + hidden
    output, normed_two, inverse_two = norm_forward(mixed_two, gains[1], shift_rows[3])
    saved = (
        whole_in, query, keys, values, attended, logsums, normed_one, inverse_one,
        whole_hidden, slope, activated, normed_two, inverse_two,
    )
    return output, saved


def own_sum(rows):
    return jnp.sum(rows[: rows.shape[0] // 2], axis=0)


def layer_backward(grad_out, saved, params, docs):
    (
        whole_in, query, keys, values, attended, logsums, normed_one, inverse_one,
        whole_hidden, slope, activated, normed_two, inverse_two,
    ) = saved
    w_proj, w_back_t, w_up, w_down_t, b_proj, b_up, gains, shift_rows = params
    width = w_back_t.shape[1]
    mixed_two_grad = norm_backward(grad_out, normed_two, inverse_two, gains[1])
    piece = core_whole(mixed_two_grad.astype(LOW))
    upper_grad = (dot(piece, w_down_t, 1, 0) * slope).astype(LOW)
    hidden_part = dot(upper_grad, w_up, 1, 1)
    hidden_grad = group_sum(hidden_part) + mixed_two_grad
    down_grad = dot(activated, piece, 0, 0)
    up_grad = dot(whole_hidden, upper_grad, 0, 0)
    mixed_one_grad = norm_backward(hidden_grad, normed_one, inverse_one, gains[0])
    piece_one = core_whole(mixed_one_grad.astype(LOW))
    attended_grad = dot(piece_one, w_back_t, 1, 0).astype(LOW)
    proj_low = attend_back(query, keys, values, attended_grad, logsums, docs)
    back_grad = dot(attended, piece_one, 0, 0)
    proj_grad = dot(proj_low, whole_in, 0, 0)
    resid_part = dot(proj_low, w_proj, 1, 1)
    bias_sums = jnp.sum(proj_low.astype(F32), axis=0)
    grads = (
        proj_grad.reshape(3, width, -1),
        back_grad,
        up_grad,
        down_grad,
        jnp.stack([bias_sums[:width], bias_sums[2 * width :]]),
        jnp.sum(upper_grad.astype(F32), axis=0),
        jnp.stack([own_sum(hidden_grad * normed_one), own_sum(grad_out * normed_two)]),
        jnp.stack([own_sum(mixed_one_grad), own_sum(hidden_grad), own_sum(mixed_two_grad), own_sum(grad_out)]),
    )
    return grads, resid_part, mixed_one_grad


def sum_over(value, axis):
    bit = 1
    while bit < lax.axis_size(axis):
        value = value + swap(value, axis, bit)
        bit *= 2
    return value


def flat_rows(parts):
    return jnp.concatenate([part.reshape(-1) for part in parts])


def sum_many(parts, axes):
    total = flat_rows(parts)
    size = total.shape[0]
    total = jnp.pad(total, (0, -size % 1024)).reshape(-1, 128)
    for axis in axes:
        total = sum_over(total, axis)
    total = total.reshape(-1)
    outs, start = [], 0
    for part in parts:
        outs.append(total[start : start + part.size].reshape(part.shape))
        start += part.size
    return outs


def first_factors(totals, starts):
    mt_proj, m_back, m_up, m_down = totals
    s_proj, s_back, s_up, s_down = starts
    return [
        jnp.einsum("jnm,jrn->jrm", mt_proj, s_proj, precision=HIGHEST),
        dot(s_back, m_back, 1, 1, HIGHEST),
        dot(s_up, m_up, 1, 1, HIGHEST),
        dot(s_down, m_down, 1, 1, HIGHEST),
    ]


def second_factors(totals, bases):
    mt_proj, m_back, m_up, m_down = totals
    p_proj, p_back, p_up, p_down = bases
    return [
        jnp.einsum("jnm,jrm->jrn", mt_proj, p_proj, precision=HIGHEST),
        dot(p_back, m_back, 1, 0, HIGHEST),
        dot(p_up, m_up, 1, 0, HIGHEST),
        dot(p_down, m_down, 1, 0, HIGHEST),
    ]


def flip(value):
    return jnp.swapaxes(value, -1, -2)


def per_device(
    x_in, out_grad, doc_lengths, keep_layer, w_qkv, w_o, w_in, w_out, b_qv, b_in, ln_gain, shifts,
    m_qkv, m_o, m_in, m_out, m_qv, m_bin, m_gain, m_shift, e_qkv, e_o, e_in, e_out, q_qkv, q_o, q_in, q_out,
):
    own_rows = x_in.shape[0]
    replicas = lax.axis_size("dp")
    index = lax.axis_index("dp")
    place = lax.axis_index("mp")
    width = w_o.shape[1]

    def gather(piece):
        return lax.all_gather(piece, "dp", axis=0, tiled=True)

    def pieces(layer):
        return (
            jnp.concatenate([w_qkv[layer, 0], w_qkv[layer, 1], w_qkv[layer, 2], flip(w_o[layer])], axis=1).astype(LOW),
            w_in[layer].astype(LOW),
            flip(w_out[layer]).astype(LOW),
        )

    order = [0, 2, 1, 3]
    places = jnp.concatenate([(place ^ v) * own_rows + jnp.arange(own_rows) for v in order])
    docs = doc_index(doc_lengths[0], places)

    one = [gather(piece) for piece in pieces(0)]
    two = [gather(piece) for piece in pieces(1)]

    def params_of(layer, whole):
        b_proj = jnp.concatenate([b_qv[layer, 0], jnp.zeros((width,), F32), b_qv[layer, 1]])
        return (
            whole[0][:, : 3 * width], whole[0][:, 3 * width :], whole[1], whole[2],
            b_proj, b_in[layer], ln_gain[layer], shifts[layer],
        )

    set_in = jnp.concatenate([x_in, swap(x_in, "mp", 2)], axis=0)
    set_grad = jnp.concatenate([out_grad, swap(out_grad, "mp", 2)], axis=0)
    layer_one = params_of(0, one)
    layer_two = params_of(1, two)
    first, saved_one = layer_forward(set_in.astype(F32), core_whole(set_in), layer_one, docs)
    second, saved_two = layer_forward(first, core_whole(first.astype(LOW)), layer_two, docs)
    keep = keep_layer[0] > 0
    output = jnp.where(keep, second[:own_rows], first[:own_rows])
    grad = set_grad.astype(F32)
    grads_two, part_two, rest_two = layer_backward(jnp.where(keep, grad, 0.0), saved_two, layer_two, docs)
    back_two = group_sum(part_two) + rest_two

    errors = (flip(e_qkv[0]), e_o[0], e_in[0], e_out[0])
    starts = tuple(flip(q) for q in (q_qkv, q_o, q_in, q_out))

    def totals_of(grads, layer):
        return [grads[member] + errors[member][layer] for member in range(4)]

    def starts_of(layer):
        return [start[layer] for start in starts]

    totals_two = totals_of(grads_two, 1)
    firsts_two = first_factors(totals_two, starts_of(1))
    sums_two = sum_many(firsts_two + [grads_two[4], grads_two[5]], ("dp",))
    bases_two = [orthogonal_rows(f) for f in sums_two[:4]]
    seconds_two = second_factors(totals_two, bases_two)

    grads_one, part_one, rest_one = layer_backward(jnp.where(keep, back_two, grad), saved_one, layer_one, docs)
    last = core_sum(part_one)
    back_one = last[:own_rows] + swap(last[own_rows:].astype(LOW), "mp", 2).astype(F32) + rest_one[:own_rows]

    totals_one = totals_of(grads_one, 0)
    firsts_one = first_factors(totals_one, starts_of(0))
    sums_one = sum_many(firsts_one + [grads_one[4], grads_one[5]] + seconds_two, ("dp",))
    bases_one = [orthogonal_rows(f) for f in sums_one[:4]]
    seconds_one = second_factors(totals_one, bases_one)
    sums_last = sum_many(seconds_one, ("dp",))
    wide = [jnp.stack([grads_one[6], grads_two[6]]), jnp.stack([grads_one[7], grads_two[7]])]
    gain_sum, shift_sum = sum_many(wide, ("mp", "dp"))

    bases = (bases_one, bases_two)
    seconds = (sums_last, sums_one[6:])
    totals = (totals_one, totals_two)
    member_errors = []
    scaled = [[second / replicas for second in seconds[layer]] for layer in range(2)]

    def approx_of(layer, member):
        base, second = bases[layer][member], scaled[layer][member]
        if member == 0:
            return jnp.einsum("jrn,jrm->jnm", second, base, precision=HIGHEST)
        return dot(base, second, 0, 0, HIGHEST)

    for member in range(4):
        member_errors.append(
            jnp.stack([totals[layer][member] - approx_of(layer, member) for layer in range(2)])[None]
        )
    member_errors[0] = flip(member_errors[0])

    def part_of(value, axis):
        rows = value.shape[axis] // replicas
        return lax.dynamic_slice_in_dim(value, index * rows, rows, axis)

    def update_qkv(layer):
        base = part_of(bases[layer][0], 2)
        return jnp.einsum("jrm,jrn->jmn", base, scaled[layer][0], precision=HIGHEST)

    def update_o(layer):
        return dot(bases[layer][1], part_of(scaled[layer][1], 1), 0, 0, HIGHEST)

    def update_in(layer):
        return dot(part_of(bases[layer][2], 1), scaled[layer][2], 0, 0, HIGHEST)

    def update_out(layer):
        return flip(dot(part_of(scaled[layer][3], 1), bases[layer][3], 0, 0, HIGHEST))

    def renew(weight, moment, update):
        moment_new = MOMENTUM * moment + jnp.stack([update(0), update(1)])
        return weight - RATE * moment_new, moment_new

    new_w_qkv, new_m_qkv = renew(w_qkv, m_qkv, update_qkv)
    new_w_o, new_m_o = renew(w_o, m_o, update_o)
    new_w_in, new_m_in = renew(w_in, m_in, update_in)
    new_w_out, new_m_out = renew(w_out, m_out, update_out)
    new_m_qv = MOMENTUM * m_qv + jnp.stack([sums_one[4], sums_two[4]]) / replicas
    new_m_bin = MOMENTUM * m_bin + jnp.stack([sums_one[5], sums_two[5]]) / replicas
    new_m_gain = MOMENTUM * m_gain + gain_sum / replicas
    new_m_shift = MOMENTUM * m_shift + shift_sum / replicas
    outer = [flip(jnp.stack([bases_one[member], bases_two[member]])) for member in range(4)]
    inner = [flip(jnp.stack([seconds[0][member], seconds[1][member]])) for member in range(4)]
    return (
        output, back_one, new_w_qkv, new_w_o, new_w_in, new_w_out,
        b_qv - RATE * new_m_qv, b_in - RATE * new_m_bin, ln_gain - RATE * new_m_gain, shifts - RATE * new_m_shift,
        new_m_qkv, new_m_o, new_m_in, new_m_out, new_m_qv, new_m_bin, new_m_gain, new_m_shift,
        *member_errors, *outer, *inner,
    )


def solution(mesh):
    in_specs = (
        P(("dp", "mp"), None), P(("dp", "mp"), None), P("dp", None), P("dp"),
        P(None, None, "dp", "mp"), P(None, "mp", "dp"), P(None, "dp", "mp"), P(None, "mp", "dp"),
        P(None, None, "mp"), P(None, "mp"), P(), P(),
        P(None, None, "dp", "mp"), P(None, "mp", "dp"), P(None, "dp", "mp"), P(None, "mp", "dp"),
        P(None, None, "mp"), P(None, "mp"), P(), P(),
        P("dp", None, None, None, "mp"), P("dp", None, "mp", None), P("dp", None, None, "mp"), P("dp", None, "mp", None),
        P(None, None, "mp", None), P(None, "mp", None), P(None, "mp", None), P(None, "mp", None),
    )
    out_specs = (
        P(("dp", "mp"), None), P(("dp", "mp"), None),
        P(None, None, "dp", "mp"), P(None, "mp", "dp"), P(None, "dp", "mp"), P(None, "mp", "dp"),
        P(None, None, "mp"), P(None, "mp"), P(), P(),
        P(None, None, "dp", "mp"), P(None, "mp", "dp"), P(None, "dp", "mp"), P(None, "mp", "dp"),
        P(None, None, "mp"), P(None, "mp"), P(), P(),
        P("dp", None, None, None, "mp"), P("dp", None, "mp", None), P("dp", None, None, "mp"), P("dp", None, "mp", None),
        P(None, None, "mp", None), P(None, "mp", None), P(None, "mp", None), P(None, "mp", None),
        P(None, None, "mp", None), P(None, "mp", None), P(None, "mp", None), P(None, "mp", None),
    )
    return jax.shard_map(per_device, mesh=mesh, in_specs=in_specs, out_specs=out_specs, check_vma=False)
```

time: 1100 us -> 849 us (0.77)
  waiting for transfers between devices: 632 us -> 277 us
  other arithmetic: 104 us -> 182 us
  blocking collectives: 75.1 us -> 0 us
  starting transfers between devices: 2.34 us -> 44.8 us
  between operations: 17.5 us -> 51.8 us
  local copies, waits for them, and re-layouts: 67.4 us -> 95 us
    reduce_scatter x8 -> x0, waiting for transfers between devices: 252 us -> none  [the longest x4 147 us: reduce_rows(): lax.psum_scatter(jnp.dot(acts_low, weight, preferred_element_type=jnp.flo...]
    ppermute x0 -> x40, waiting for transfers between devices: none -> 148 us  [swap(): return lax.ppermute(value, axis, [(i, i ^ bit) for i in range(size)])]
    all_gather x11 -> x6, waiting for transfers between devices: 256 us -> 129 us  [gather(): return lax.all_gather(piece, 'dp', axis=0, tiled=True)]
    psum x3 -> x0, waiting for transfers between devices: 123 us -> none  [the longest x2 108 us: sum_bucket_first(): lax.psum((parts[0], parts[1], parts[2], parts[3], parts[4], parts[5]), 'dp')]
    reduce_sum x75 -> x140, other arithmetic: 30.8 us -> 77.9 us  [the longest x62 37.2 us: orthogonal_rows(): jnp.sum(vector * vector, axis=-1, keepdims=True) + ORTHO_EPS]
    psum x1 -> x0, blocking collectives: 40.1 us -> none  [per_device(): lax.psum((jnp.stack([grads_one[6], grads_two[6]]), jnp.stack([grads_one[7...]
    all_gather x1 -> x0, blocking collectives: 35 us -> none  [per_device(): lax.all_gather(w_o.astype(jnp.bfloat16), 'dp', axis=2, tiled=True)]
    ppermute x0 -> x40, starting transfers between devices: none -> 32.2 us  [swap(): return lax.ppermute(value, axis, [(i, i ^ bit) for i in range(size)])]
  transfers between devices with their start and end apart: 22 -> 46, of which waited for: 20 -> 33; matrix products, arithmetic and copies ran while one was open for 13% -> 35% of each run, Pallas kernels for 0% -> 0%
where the time goes in v1:
time: 849 us; the launch traced here: 837 us
  waiting for transfers between devices  277 us (33%)
  matrix products  186 us (22%)
  other arithmetic  182 us (21%)
  local copies, waits for them, and re-layouts  95 us (11%)
  between operations  51.8 us (6%)
  starting transfers between devices  44.8 us (5%)
    dot_general x84, matrix products, dot(): lax.dot_general(left, right, (((left_dim,), (right_dim,)), ((), ())), pre...  166 us
    ppermute x40, waiting for transfers between devices, swap(): return lax.ppermute(value, axis, [(i, i ^ bit) for i in range(size)])  148 us
    all_gather x6, waiting for transfers between devices, gather(): return lax.all_gather(piece, 'dp', axis=0, tiled=True)  129 us
    unnamed x555, local copies, waits for them, and re-layouts  49.3 us
    reduce_sum x62, other arithmetic, orthogonal_rows(): jnp.sum(vector * vector, axis=-1, keepdims=True) + ORTHO_EPS  37.2 us
    ppermute x40, starting transfers between devices, swap(): return lax.ppermute(value, axis, [(i, i ^ bit) for i in range(size)])  32.2 us
    reduce_sum x56, other arithmetic, orthogonal_rows(): factor = remain - vector * jnp.sum(vector * remain, axis=-1, keepdims=True)  22.6 us
    mul x52, other arithmetic, orthogonal_rows(): vector * lax.rsqrt(jnp.sum(vector * vector, axis=-1, keepdims=True) + ORT...  17.9 us
  transfers between devices with their start and end apart: 46, of which 33 were waited for; matrix products, arithmetic and copies ran while one was open for 35% of the time, Pallas kernels for 0%

profile of v1, /device:TPU:0, one launch (start us, length us, event | category | flops | bytes accessed | tf_op | source)
XLA Modules:
  0.0 836.6 jit_solution(15380084187161521542)
XLA Ops:
  15.1 7.4 collective-permute-done
  26.5 28.1 %all-gather.9.cloned.1.call-done = bf16[768,768]{1,0:T(8,128)(2,1)} async-done(((bf16[96,768]{1,0:T(8,128)(2,1)}), bf16[768,768]{1,0:T(8,128)(2,1)}) %all-gather.9.cloned.1.call-update) | async-done | bytes 1179664 | tf_op jit(solution)/shard_map/all_gather | solution.py:258
  72.1 12.4 %all-gather.13.cloned.1.call-start = ((), (), s32[]{:S(2)}) async-start(), calls=%async_computation.2 | async-start | bytes 1327104 | tf_op jit(solution)/shard_map/all_gather | solution.py:258
  85.7 3.7 collective-permute-done.3
  92.5 4.7 all-gather.17.cloned.1.call-done
  97.2 5.4 multiply_convert_fusion.7
  102.6 37.2 %all-gather.11.cloned.1.call-done = bf16[768,768]{1,0:T(8,128)(2,1)} async-done(((bf16[96,768]{1,0:T(8,128)(2,1)}), bf16[768,768]{1,0:T(8,128)(2,1)}) %all-gather.11.cloned.1.call-update) | async-done | bytes 1179664 | tf_op jit(solution)/shard_map/all_gather | solution.py:258
  139.8 3.2 fusion.270
  148.8 17.5 %collective-permute-done.6 = bf16[512,768]{1,0:T(8,128)(2,1)S(1)} collective-permute-done((bf16[512,768]{1,0:T(8,128)(2,1)}, bf16[512,768]{1,0:T(8,128)(2,1)S(1)}, u32[]{:S(2)}, u32[]{:S(2)}) %collective-permute-start.6) | collective-permute-done | bytes 786464 | tf_op jit(solution)/shard_map/ppermute | solution.py:33
  169.1 18.8 %all-gather.13.cloned.1.call-done = bf16[768,768]{1,0:T(8,128)(2,1)} async-done(((bf16[96,768]{1,0:T(8,128)(2,1)}), bf16[768,768]{1,0:T(8,128)(2,1)}) %all-gather.13.cloned.1.call-update) | async-done | bytes 1179664 | tf_op jit(solution)/shard_map/all_gather | solution.py:258
  204.6 18.4 %collective-permute-done.9 = bf16[512,768]{1,0:T(8,128)(2,1)} collective-permute-done((bf16[512,768]{1,0:T(8,128)(2,1)}, bf16[512,768]{1,0:T(8,128)(2,1)}, u32[]{:S(2)}, u32[]{:S(2)}) %collective-permute-start.9) | collective-permute-done | bytes 786464 | tf_op jit(solution)/shard_map/ppermute | solution.py:33
  227.3 3.1 all-gather.19.cloned.1.call-done
  230.4 5.5 multiply_convert_fusion.6
  235.9 37.0 %all-gather.15.cloned.1.call-done = bf16[768,768]{1,0:T(8,128)(2,1)} async-done(((bf16[96,768]{1,0:T(8,128)(2,1)}), bf16[768,768]{1,0:T(8,128)(2,1)}) %all-gather.15.cloned.1.call-update) | async-done | bytes 1179664 | tf_op jit(solution)/shard_map/all_gather | solution.py:258
  272.9 3.2 fusion.271
  281.8 17.7 %collective-permute-done.12 = bf16[512,768]{1,0:T(8,128)(2,1)S(1)} collective-permute-done((bf16[512,768]{1,0:T(8,128)(2,1)S(1)}, bf16[512,768]{1,0:T(8,128)(2,1)S(1)}, u32[]{:S(2)}, u32[]{:S(2)}) %collective-permute-start.12) | collective-permute-done | bytes 786464 | tf_op jit(solution)/shard_map/ppermute | solution.py:33
  300.5 6.7 collective-permute-done.13
  312.4 3.8 convert_reduce_fusion
  329.0 3.6 bitcast_add_fusion
  338.0 7.7 collective-permute-done.16
  352.0 3.6 bitcast_add_fusion.1
  365.9 4.5 multiply_reduce_fusion.3
  370.4 3.4 multiply_reduce_fusion.4
  373.8 3.6 multiply_reduce_fusion.5
  382.7 4.8 multiply_convert_fusion.5
  413.6 4.7 collective-permute-done.26
  546.6 13.7 %collective-permute-done.19 = bf16[512,768]{1,0:T(8,128)(2,1)S(1)} collective-permute-done((bf16[512,768]{1,0:T(8,128)(2,1)S(1)}, bf16[512,768]{1,0:T(8,128)(2,1)S(1)}, u32[]{:S(2)}, u32[]{:S(2)}) %collective-permute-start.19) | collective-permute-done | bytes 786464 | tf_op jit(solution)/shard_map/ppermute | solution.py:33
  569.4 5.5 convert_reduce_fusion.1
  592.8 4.3 bitcast_add_fusion.2
  597.2 7.0 collective-permute-done.22
  610.7 4.1 bitcast_add_fusion.3
  621.3 3.3 multiply_reduce_fusion
  626.9 3.1 multiply_reduce_fusion.2
  630.0 3.5 multiply_convert_fusion.2
  642.9 3.9 fusion.272
  650.4 3.1 convolution_bitcast_fusion.9
  659.2 4.9 collective-permute-done.29
  666.6 5.0 collective-permute-done.30
  674.5 3.1 fusion.84
  680.2 4.6 collective-permute-done.31
  686.8 5.1 subtract_bitcast_fusion.2
  691.9 5.3 subtract_bitcast_fusion
  699.8 4.4 subtract_bitcast_fusion.4
  756.1 3.0 fusion.204
  765.9 3.9 collective-permute-done.33
  778.4 5.1 subtract_bitcast_fusion.3
  784.8 4.3 subtract_bitcast_fusion.5
  789.6 3.9 subtract_bitcast_fusion.1
  (1187 shorter events, 411.2 us)
Async XLA Ops:
  7.2 47.4 %all-gather.9.cloned.1.call-start = ((), (), s32[]{:S(2)}) async-start(), calls=%async_computation | async-start | bytes 1327104 | tf_op jit(solution)/shard_map/all_gather | solution.py:258
  10.3 86.9 %all-gather.17.cloned.1.call-start = ((), (), s32[]{:S(2)}) async-start(), calls=%async_computation.4 | async-start | bytes 1327104 | tf_op jit(solution)/shard_map/all_gather | solution.py:258
  10.4 12.1 %collective-permute-start = (bf16[256,768]{1,0:T(8,128)(2,1)S(1)}, bf16[256,768]{1,0:T(8,128)(2,1)S(1)}, u32[]{:S(2)}, u32[]{:S(2)}) collective-permute-start(bf16[256,768]{1,0:T(8,128)(2,1)S(1)} %copy-done.121), channel_id=1, source_target_pairs={{0,2},{1,3},{2,0},{3,1},{4,6},{5,7},{6,4},{7,5},{8,10},{9,11},{10,... | collective-permute-start | bytes 1179656 | tf_op jit(solution)/shard_map/ppermute | solution.py:33
  14.2 125.6 %all-gather.11.cloned.1.call-start = ((), (), s32[]{:S(2)}) async-start(), calls=%async_computation.1 | async-start | bytes 1327104 | tf_op jit(solution)/shard_map/all_gather | solution.py:258
  23.3 2.3 collective-permute-start.1
  67.2 2.4 collective-permute-start.2
  69.8 19.6 %collective-permute-start.3 = (bf16[512,768]{1,0:T(8,128)(2,1)S(1)}, bf16[512,768]{1,0:T(8,128)(2,1)S(1)}, u32[]{:S(2)}, u32[]{:S(2)}) collective-permute-start(bf16[512,768]{1,0:T(8,128)(2,1)S(1)} %fusion.74), channel_id=1, source_target_pairs={{0,2},{1,3},{2,0},{3,1},{4,6},{5,7},{6,4},{7,5},{8,10},{9,11},{10,... | collective-permute-start | bytes 2359304 | tf_op jit(solution)/shard_map/ppermute | solution.py:33
  72.1 115.9 %all-gather.13.cloned.1.call-start = ((), (), s32[]{:S(2)}) async-start(), calls=%async_computation.2 | async-start | bytes 1327104 | tf_op jit(solution)/shard_map/all_gather | solution.py:258
  85.7 140.4 %copy-start.191 = (f32[768]{0:T(1024)}, f32[768]{0:T(1024)S(1)}, u32[]{:S(2)}) copy-start(f32[768]{0:T(1024)S(1)} %get-tuple-element.56) | copy-start | bytes 9220
  92.3 4.9 collective-permute-start.4
  92.5 137.9 %copy-start.244 = (f32[768]{0:T(1024)}, f32[768]{0:T(1024)S(1)}, u32[]{:S(2)}) copy-start(f32[768]{0:T(1024)S(1)} %get-tuple-element.66) | copy-start | bytes 9220
  143.1 2.4 collective-permute-start.5
  146.5 19.8 %collective-permute-start.6 = (bf16[512,768]{1,0:T(8,128)(2,1)}, bf16[512,768]{1,0:T(8,128)(2,1)S(1)}, u32[]{:S(2)}, u32[]{:S(2)}) collective-permute-start(bf16[512,768]{1,0:T(8,128)(2,1)} %fusion.75), channel_id=1, source_target_pairs={{0,2},{1,3},{2,0},{3,1},{4,6},{5,7},{6,4},{7,5},{8,10},{9,11},{10,... | collective-permute-start | bytes 2359304 | tf_op jit(solution)/shard_map/ppermute | solution.py:33
  148.8 81.6 %all-gather.19.cloned.1.call-start = ((), (), s32[]{:S(2)}) async-start(), calls=%async_computation.5 | async-start | bytes 1327104 | tf_op jit(solution)/shard_map/all_gather | solution.py:258
  169.1 18.9 %collective-permute-start.7 = (bf16[512,768]{1,0:T(8,128)(2,1)}, bf16[512,768]{1,0:T(8,128)(2,1)}, u32[]{:S(2)}, u32[]{:S(2)}) collective-permute-start(bf16[512,768]{1,0:T(8,128)(2,1)} %get-tuple-element.174), channel_id=1, source_target_pairs={{0,1},{1,0},{2,3},{3,2},{4,5},{5,4},{6,7},{7,6},{8,9},{9,8},{10,11... | collective-permute-start | bytes 2359304 | tf_op jit(solution)/shard_map/ppermute | solution.py:33
  169.1 103.8 %all-gather.15.cloned.1.call-start = ((), (), s32[]{:S(2)}) async-start(), calls=%async_computation.3 | async-start | bytes 1327104 | tf_op jit(solution)/shard_map/all_gather | solution.py:258
  199.6 2.4 collective-permute-start.8
  203.1 19.9 %collective-permute-start.9 = (bf16[512,768]{1,0:T(8,128)(2,1)}, bf16[512,768]{1,0:T(8,128)(2,1)}, u32[]{:S(2)}, u32[]{:S(2)}) collective-permute-start(bf16[512,768]{1,0:T(8,128)(2,1)} %fusion.76), channel_id=1, source_target_pairs={{0,2},{1,3},{2,0},{3,1},{4,6},{5,7},{6,4},{7,5},{8,10},{9,11},{10,... | collective-permute-start | bytes 2359304 | tf_op jit(solution)/shard_map/ppermute | solution.py:33
  227.3 3.1 collective-permute-start.10
  276.1 2.8 collective-permute-start.11
  279.1 20.4 %collective-permute-start.12 = (bf16[512,768]{1,0:T(8,128)(2,1)S(1)}, bf16[512,768]{1,0:T(8,128)(2,1)S(1)}, u32[]{:S(2)}, u32[]{:S(2)}) collective-permute-start(bf16[512,768]{1,0:T(8,128)(2,1)S(1)} %fusion.77), channel_id=1, source_target_pairs={{0,2},{1,3},{2,0},{3,1},{4,6},{5,7},{6,4},{7,5},{8,10},{9,11},{10,... | collective-permute-start | bytes 2359304 | tf_op jit(solution)/shard_map/ppermute | solution.py:33
  280.6 26.5 %collective-permute-start.13 = (bf16[256,768]{1,0:T(8,128)(2,1)S(1)}, bf16[256,768]{1,0:T(8,128)(2,1)S(1)}, u32[]{:S(2)}, u32[]{:S(2)}) collective-permute-start(bf16[256,768]{1,0:T(8,128)(2,1)S(1)} %copy-done.64), channel_id=1, source_target_pairs={{0,2},{1,3},{2,0},{3,1},{4,6},{5,7},{6,4},{7,5},{8,10},{9,11},{10,... | collective-permute-start | bytes 1179656 | tf_op jit(solution)/shard_map/ppermute | solution.py:33
  310.1 2.3 collective-permute-start.14
  320.3 3.0 collective-permute-start.15
  325.7 20.1 %collective-permute-start.16 = (bf16[512,768]{1,0:T(8,128)(2,1)}, bf16[512,768]{1,0:T(8,128)(2,1)}, u32[]{:S(2)}, u32[]{:S(2)}) collective-permute-start(bf16[512,768]{1,0:T(8,128)(2,1)} %fusion.78), channel_id=1, source_target_pairs={{0,2},{1,3},{2,0},{3,1},{4,6},{5,7},{6,4},{7,5},{8,10},{9,11},{10,... | collective-permute-start | bytes 2359304 | tf_op jit(solution)/shard_map/ppermute | solution.py:33
  351.3 12.3 %collective-permute-start.17 = (bf16[512,768]{1,0:T(8,128)(2,1)}, bf16[512,768]{1,0:T(8,128)(2,1)}, u32[]{:S(2)}, u32[]{:S(2)}) collective-permute-start(bf16[512,768]{1,0:T(8,128)(2,1)} %get-tuple-element.162), channel_id=1, source_target_pairs={{0,1},{1,0},{2,3},{3,2},{4,5},{5,4},{6,7},{7,6},{8,9},{9,8},{10,11... | collective-permute-start | bytes 2359304 | tf_op jit(solution)/shard_map/ppermute | solution.py:33
  412.9 5.4 collective-permute-start.26
  418.3 5.1 collective-permute-start.27
  423.4 7.4 collective-permute-start.28
  429.2 110.0 %collective-permute-start.18 = (bf16[512,768]{1,0:T(8,128)(2,1)S(1)}, bf16[512,768]{1,0:T(8,128)(2,1)S(1)}, u32[]{:S(2)}, u32[]{:S(2)}) collective-permute-start(bf16[512,768]{1,0:T(8,128)(2,1)S(1)} %slice.1899), channel_id=1, source_target_pairs={{0,1},{1,0},{2,3},{3,2},{4,5},{5,4},{6,7},{7,6},{8,9},{9,8},{10,11... | collective-permute-start | bytes 2359304 | tf_op jit(solution)/shard_map/ppermute | solution.py:33
  541.8 18.5 %collective-permute-start.19 = (bf16[512,768]{1,0:T(8,128)(2,1)S(1)}, bf16[512,768]{1,0:T(8,128)(2,1)S(1)}, u32[]{:S(2)}, u32[]{:S(2)}) collective-permute-start(bf16[512,768]{1,0:T(8,128)(2,1)S(1)} %fusion.79), channel_id=1, source_target_pairs={{0,2},{1,3},{2,0},{3,1},{4,6},{5,7},{6,4},{7,5},{8,10},{9,11},{10,... | collective-permute-start | bytes 2359304 | tf_op jit(solution)/shard_map/ppermute | solution.py:33
  564.5 4.8 collective-permute-start.20
  577.5 5.2 collective-permute-start.21
  583.9 20.3 %collective-permute-start.22 = (bf16[512,768]{1,0:T(8,128)(2,1)}, bf16[512,768]{1,0:T(8,128)(2,1)}, u32[]{:S(2)}, u32[]{:S(2)}) collective-permute-start(bf16[512,768]{1,0:T(8,128)(2,1)} %fusion.80), channel_id=1, source_target_pairs={{0,2},{1,3},{2,0},{3,1},{4,6},{5,7},{6,4},{7,5},{8,10},{9,11},{10,... | collective-permute-start | bytes 2359304 | tf_op jit(solution)/shard_map/ppermute | solution.py:33
  608.0 10.9 %collective-permute-start.23 = (bf16[512,768]{1,0:T(8,128)(2,1)}, bf16[512,768]{1,0:T(8,128)(2,1)}, u32[]{:S(2)}, u32[]{:S(2)}) collective-permute-start(bf16[512,768]{1,0:T(8,128)(2,1)} %get-tuple-element.156), channel_id=1, source_target_pairs={{0,1},{1,0},{2,3},{3,2},{4,5},{5,4},{6,7},{7,6},{8,9},{9,8},{10,11... | collective-permute-start | bytes 2359304 | tf_op jit(solution)/shard_map/ppermute | solution.py:33
  656.0 8.1 collective-permute-start.29
  664.1 7.4 collective-permute-start.30
  672.6 12.2 %collective-permute-start.31 = (f32[448,128]{1,0:T(8,128)S(1)}, f32[448,128]{1,0:T(8,128)S(1)}, u32[]{:S(2)}, u32[]{:S(2)}) collective-permute-start(f32[448,128]{1,0:T(8,128)S(1)} %fusion.355), channel_id=1, source_target_pairs={{0,16},{4,20},{8,24},{12,28},{16,0},{20,4},{24,8},{28,12},{1,17},{... | collective-permute-start | bytes 688136 | tf_op jit(solution)/shard_map/ppermute | solution.py:33
  680.2 90.4 %collective-permute-start.24 = (bf16[512,768]{1,0:T(8,128)(2,1)}, bf16[512,768]{1,0:T(8,128)(2,1)}, u32[]{:S(2)}, u32[]{:S(2)}) collective-permute-start(bf16[512,768]{1,0:T(8,128)(2,1)} %slice.1897), channel_id=1, source_target_pairs={{0,1},{1,0},{2,3},{3,2},{4,5},{5,4},{6,7},{7,6},{8,9},{9,8},{10,11... | collective-permute-start | bytes 2359304 | tf_op jit(solution)/shard_map/ppermute | solution.py:33
  760.5 4.6 collective-permute-start.32
  765.2 4.6 collective-permute-start.33
  769.8 6.0 collective-permute-start.34
  774.3 33.0 %collective-permute-start.25 = (bf16[256,768]{1,0:T(8,128)(2,1)}, bf16[256,768]{1,0:T(8,128)(2,1)}, u32[]{:S(2)}, u32[]{:S(2)}) collective-permute-start(bf16[256,768]{1,0:T(8,128)(2,1)} %slice.1905), channel_id=1, source_target_pairs={{0,2},{1,3},{2,0},{3,1},{4,6},{5,7},{6,4},{7,5},{8,10},{9,11},{10,... | collective-permute-start | bytes 1179656 | tf_op jit(solution)/shard_map/ppermute | solution.py:33
  810.1 1.3 collective-permute-start.35
  811.4 4.0 collective-permute-start.36
  815.4 4.0 collective-permute-start.37
  819.4 4.0 collective-permute-start.38
  823.4 4.9 collective-permute-start.39
  (260 other events, 1448.2 us)
Sparse Core Ops, SparseCore 0:
  10.8 43.7 all-gather.8
  57.3 39.8 all-gather.16
  100.0 39.8 all-gather.10
  148.9 38.9 all-gather.12
  190.5 39.8 all-gather.18
  233.0 39.8 all-gather.14
